TPU v7x, 128 devices: a whole 4x4x4 slice. The times are simulated.
128 devices in a mesh: rep: 8 (over y_hi, z), fsdp: 16 (over y_lo, x, core).
Axes of the slice: x: 4, y: 4 (y_hi: 2, y_lo: 2; y = y_hi * 2 + y_lo), z: 4, core: 2. Of those that a mesh axis runs over, the one named last changes fastest.
Arguments:
- attn_out: bfloat16 [8, 4096, 2560], P('rep', 'fsdp'), may hold values from -6 to 6
- residual: bfloat16 [8, 4096, 5120], P('rep', 'fsdp'), may hold values from -400 to 400
- cotangent: bfloat16 [8, 4096, 5120], P('rep', 'fsdp'), may hold values from -2 to 2
- norm_gain: bfloat16 [5120], P('fsdp'), may hold values from 0.29882812 to 3
- params: float32 [8, 5120, 2560], P('rep', 'fsdp'), may hold values from -1 to 1
- first_moment: float32 [8, 5120, 2560], P('rep', 'fsdp'), may hold values from -3 to 3
- second_moment: float32 [8, 5120, 2560], P('rep', 'fsdp'), may hold values from 0.05 to 2
- step_count: int32 [1], replicated, may hold values from 0 to 63
Outputs:
- params_out: float32 [8, 5120, 2560], P('rep', 'fsdp')
- first_out: float32 [8, 5120, 2560], P('rep', 'fsdp')
- second_out: float32 [8, 5120, 2560], P('rep', 'fsdp')
All inputs are finite; a program needn't handle non-finite values.
Results may differ from a plain program's by a relative error of at most 0.007.
Values may be sent and summed in bfloat16 or wider, within the bound.
A program may use at most 192 MiB of HBM per device.

v0:
```python
from functools import partial
import jax
import jax.numpy as jnp
from jax import lax
from jax.sharding import PartitionSpec as P

beta_one = 0.9
beta_two = 0.999
learn_rate = 0.001
decay_rate = 0.1
norm_eps = 1e-05
adam_eps = 1e-08


def partner(value, axis, bit):
    mask = 2**bit
    pairs = [(source, source ^ mask) for source in range(lax.axis_size(axis))]
    return lax.ppermute(value, axis, pairs)


def norm_backward(pre_norm, scaled, square_sum, cross_sum, width_total):
    inv_rms = lax.rsqrt(square_sum / width_total + norm_eps)
    correction = inv_rms * inv_rms * inv_rms * cross_sum / width_total
    return (inv_rms[:, None] * scaled - pre_norm * correction[:, None]).astype(jnp.bfloat16)


def adam_change(params_local, gradient, first_local, second_local, step_count):
    step_time = (step_count[0] + 1).astype(jnp.float32)
    first_fix = 1.0 - jnp.power(jnp.float32(beta_one), step_time)
    second_fix = 1.0 - jnp.power(jnp.float32(beta_two), step_time)
    first_new = beta_one * first_local + (1.0 - beta_one) * gradient
    second_new = beta_two * second_local + (1.0 - beta_two) * gradient * gradient
    update_step = -learn_rate * (
        first_new / first_fix / (jnp.sqrt(second_new / second_fix) + adam_eps)
        + decay_rate * params_local
    )
    return (update_step, first_new, second_new)


def swap_updated(shard_data, bit_number):
    return partner(shard_data, "rep", bit_number)


def pick_partner(shard_data, partner_level, helper, level_count):
    branches = [partial(helper, bit_number=number) for number in range(level_count)]
    return lax.switch(partner_level, branches, shard_data)


def per_device(
    attn_out, residual, cotangent, norm_gain, params, first_moment, second_moment, step_count
):
    local_attn = attn_out[0]
    width_total = residual.shape[2]
    params_local = params[0]
    w_half = params_local.astype(jnp.bfloat16)
    contract_feat = (((1,), (1,)), ((), ()))
    contract_rows = (((0,), (0,)), ((), ()))
    full_attn = lax.all_gather(local_attn, "fsdp", axis=0, tiled=True)
    pre_cols = lax.dot_general(full_attn, w_half, contract_feat, preferred_element_type=jnp.float32)
    resid_cols, cotan_cols = (
        lax.all_to_all(residual[0], "fsdp", split_axis=1, concat_axis=0, tiled=True),
        lax.all_to_all(cotangent[0], "fsdp", split_axis=1, concat_axis=0, tiled=True),
    )
    pre_norm = resid_cols.astype(jnp.float32) + pre_cols
    scaled = norm_gain.astype(jnp.float32)[None, :] * cotan_cols.astype(jnp.float32)
    square_sum, cross_sum = (
        lax.psum(jnp.sum(pre_norm * pre_norm, axis=1).astype(jnp.bfloat16), "fsdp").astype(
            jnp.float32
        ),
        lax.psum(jnp.sum(pre_norm * scaled, axis=1).astype(jnp.bfloat16), "fsdp").astype(
            jnp.float32
        ),
    )
    grad_pre = norm_backward(pre_norm, scaled, square_sum, cross_sum, width_total)
    gradient = lax.dot_general(
        grad_pre, full_attn, contract_rows, preferred_element_type=jnp.float32
    )
    update_step, first_new, second_new = adam_change(
        params_local, gradient, first_moment[0], second_moment[0], step_count
    )
    level_count = lax.axis_size("rep").bit_length() - 1
    partner_level = jnp.remainder(step_count[0], level_count)
    updated = params_local + update_step
    updated_far = pick_partner(updated, partner_level, swap_updated, level_count)
    params_change = 0.5 * (updated_far - params_local) + 0.5 * update_step
    return (params_change[None], first_new[None], second_new[None])


def solution(mesh):
    return jax.shard_map(
        per_device,
        mesh=mesh,
        in_specs=(
            P("rep", "fsdp", None),
            P("rep", "fsdp", None),
            P("rep", "fsdp", None),
            P("fsdp"),
            P("rep", "fsdp", None),
            P("rep", "fsdp", None),
            P("rep", "fsdp", None),
            P(),
        ),
        out_specs=(P("rep", "fsdp", None), P("rep", "fsdp", None), P("rep", "fsdp", None)),
        check_vma=False,
    )
```

profile of v0, /device:TPU:0, one launch (start us, length us, event | category | flops | bytes accessed | tf_op | source)
XLA Modules:
  0.0 361.3 jit_solution(13053667947359435022)
XLA Ops:
  7.2 0.0 all-gather.3.cloned.1.call-start
  7.2 0.7 all-gather.3.cloned.1.call-update
  7.9 4.4 %copy.13 = bf16[1,256,5120]{1,2,0:T(8,128)(2,1)} copy(bf16[1,256,5120]{2,1,0:T(8,128)(2,1)} %param.12) | data formatting | bytes 5242880 | tf_op args[1]
  12.3 5.5 %all-to-all-start = ((bf16[256,16,320]{0,2,1:T(8,128)(2,1)}), bf16[256,16,320]{0,2,1:T(8,128)(2,1)S(1)}, u32[]{:S(2)}, u32[]{:S(2)}) async-start(bf16[256,16,320]{0,2,1:T(8,128)(2,1)} %bitcast.3), calls=%async_computation | async-start | bytes 5242880 | tf_op jit(solution)/shard_map/all_to_all | solution.py:61
  17.8 4.4 %copy.15 = bf16[1,256,5120]{1,2,0:T(8,128)(2,1)} copy(bf16[1,256,5120]{2,1,0:T(8,128)(2,1)} %param.13) | data formatting | bytes 5242880 | tf_op args[2]
  22.2 0.0 copy-start.1
  22.2 51.5 %all-to-all-done = bf16[256,16,320]{0,2,1:T(8,128)(2,1)S(1)} async-done(((bf16[256,16,320]{0,2,1:T(8,128)(2,1)}), bf16[256,16,320]{0,2,1:T(8,128)(2,1)S(1)}, u32[]{:S(2)}, u32[]{:S(2)}) %all-to-all-start) | async-done | bytes 2621472 | tf_op jit(solution)/shard_map/all_to_all | solution.py:61
  73.7 6.6 %all-to-all-start.1 = ((bf16[256,16,320]{0,2,1:T(8,128)(2,1)}), bf16[256,16,320]{0,2,1:T(8,128)(2,1)}, u32[]{:S(2)}, u32[]{:S(2)}) async-start(bf16[256,16,320]{0,2,1:T(8,128)(2,1)} %bitcast.6), calls=%async_computation.1 | async-start | bytes 5242880 | tf_op jit(solution)/shard_map/all_to_all | solution.py:62
  81.0 0.0 copy-done.1
  81.1 0.6 convert_bitcast_fusion.1
  81.6 3.0 copy.17
  84.6 55.3 %all-to-all-done.1 = bf16[256,16,320]{0,2,1:T(8,128)(2,1)} async-done(((bf16[256,16,320]{0,2,1:T(8,128)(2,1)}), bf16[256,16,320]{0,2,1:T(8,128)(2,1)}, u32[]{:S(2)}, u32[]{:S(2)}) %all-to-all-start.1) | async-done | bytes 2621472 | tf_op jit(solution)/shard_map/all_to_all | solution.py:62
  139.9 2.3 convert_bitcast_fusion
  142.3 0.0 copy-start
  142.3 3.0 copy.18
  145.2 32.3 %all-gather.3.cloned.1.call-done = bf16[1,4096,2560]{2,1,0:T(8,128)(2,1)} async-done(((bf16[1,256,2560]{2,1,0:T(8,128)(2,1)}), bf16[1,4096,2560]{2,1,0:T(8,128)(2,1)}) %all-gather.3.cloned.1.call-update) | async-done | bytes 20971536 | tf_op jit(solution)/shard_map/all_gather | solution.py:58
  177.5 0.0 copy-done
  177.5 24.1 %multiply_reduce_fusion.1 = (bf16[4096]{0:T(1024)(128)(2,1)S(1)}, bf16[4096]{0:T(1024)(128)(2,1)S(1)}, f32[4096,320]{0,1:T(8,128)}) fusion(f32[4096,320]{0,1:T(8,128)} %bitcast.77, f32[320]{0:T(512)S(1)} %convert_element_type.49, f32[4096,320]{0,1:T(8,128)} %bitcast.79, bf16[1,4096,2560]{2,1,0:T(8,128)(2,1)} %all-gather.3.cloned.1.call-done, ...), kind=kOutput, calls=%fused_computation.9 | convolution fusion | flops 6718742528 | bytes 39994624 | tf_op jit(solution)/shard_map/dot_general | solution.py:59
  201.6 55.2 %all-reduce = (bf16[4096]{0:T(1024)(128)(2,1)S(1)}, bf16[4096]{0:T(1024)(128)(2,1)S(1)}) all-reduce(bf16[4096]{0:T(1024)(128)(2,1)S(1)} %get-tuple-element.11, bf16[4096]{0:T(1024)(128)(2,1)S(1)} %get-tuple-element.10), channel_id=1, replica_groups=mesh['rep'=8,'fsdp'=16] {'fsdp'}, use_global_device_ids=true, to_apply=%region_3.0 | all-reduce | flops 8192 | bytes 32768 | tf_op jit(solution)/shard_map/psum | solution.py:70
  256.9 19.5 %bitcast_add_fusion.1 = (f32[320,2560]{1,0:T(8,128)}, f32[320,2560]{1,0:T(8,128)}) fusion(f32[1,320,2560]{2,1,0:T(8,128)S(1)} %copy-done, f32[]{:T(128)} %bitcast.10, f32[1,320,2560]{2,1,0:T(8,128)} %param.17, f32[]{:T(128)} %bitcast.8, f32[1,320,2560]{2,1,0:T(8,128)} %param.16, bf16[1,4096,2560]{2,1,0:T(8,128)(2,1)} %all-gather.3.cloned.1.call-done, ...), kind=kOutput, calls=%fused_computation.14 | convolution fusion | flops 6729728000 | bytes 47875336 | tf_op jit(solution)/shard_map/dot_general | solution.py:75
  276.4 69.4 %conditional.1 = (f32[320,2560]{1,0:T(8,128)}) conditional(s32[]{:T(128)} %clamp.3, f32[320,2560]{1,0:T(8,128)} %get-tuple-element.20, f32[320,2560]{1,0:T(8,128)} %get-tuple-element.20, f32[320,2560]{1,0:T(8,128)} %get-tuple-element.20), branch_computations={%region_4.5_spmd, %region_5.6_spmd, %region_6.7_spmd} | conditional | bytes 13107248 | solution.py:46
  276.4 1.9 collective-permute-start
  278.3 67.5 %collective-permute-done = f32[320,2560]{1,0:T(8,128)} collective-permute-done((f32[320,2560]{1,0:T(8,128)}, f32[320,2560]{1,0:T(8,128)}, u32[]{:S(2)}, u32[]{:S(2)}) %collective-permute-start) | collective-permute-done | bytes 3276832 | tf_op jit(solution)/shard_map/cond/branch_0_fun/ppermute | solution.py:18
  345.8 8.7 %fusion.16 = (f32[1,320,2560]{2,1,0:T(8,128)}, f32[1,320,2560]{2,1,0:T(8,128)}, f32[1,320,2560]{2,1,0:T(8,128)}) fusion(f32[320,2560]{1,0:T(8,128)} %get-tuple-element.21, f32[1,320,2560]{2,1,0:T(8,128)} %param.17, f32[]{:T(128)} %bitcast.10, f32[]{:T(128)} %bitcast.8, f32[1,320,2560]{2,1,0:T(8,128)} %param.16, f32[320,2560]{1,0:T(8,128)} %get-tuple-element.22, ...), kind=kLoop, calls=%fused_computation.25 | loop fusion | flops 13926400 | bytes 26214408 | tf_op jit(solution)/shard_map/broadcast_in_dim | solution.py:86
  (2 shorter events, 0.0 us)
Async XLA Ops:
  7.2 170.3 %all-gather.3.cloned.1.call-start = ((), (), s32[]{:S(2)}) async-start(), calls=%async_computation.2 | async-start | bytes 22282240 | tf_op jit(solution)/shard_map/all_gather | solution.py:58
  12.3 61.4 %all-to-all-start = ((bf16[256,16,320]{0,2,1:T(8,128)(2,1)}), bf16[256,16,320]{0,2,1:T(8,128)(2,1)S(1)}, u32[]{:S(2)}, u32[]{:S(2)}) async-start(bf16[256,16,320]{0,2,1:T(8,128)(2,1)} %bitcast.3), calls=%async_computation | async-start | bytes 5242880 | tf_op jit(solution)/shard_map/all_to_all | solution.py:61
  22.2 58.8 %copy-start.1 = (bf16[320]{0:T(512)(128)(2,1)S(1)}, bf16[320]{0:T(512)(128)(2,1)}, u32[]{:S(2)}) copy-start(bf16[320]{0:T(512)(128)(2,1)} %param.14) | copy-start | bytes 1924
  73.7 66.3 %all-to-all-start.1 = ((bf16[256,16,320]{0,2,1:T(8,128)(2,1)}), bf16[256,16,320]{0,2,1:T(8,128)(2,1)}, u32[]{:S(2)}, u32[]{:S(2)}) async-start(bf16[256,16,320]{0,2,1:T(8,128)(2,1)} %bitcast.6), calls=%async_computation.1 | async-start | bytes 5242880 | tf_op jit(solution)/shard_map/all_to_all | solution.py:62
  142.3 35.3 %copy-start = (f32[1,320,2560]{2,1,0:T(8,128)S(1)}, f32[1,320,2560]{2,1,0:T(8,128)}, u32[]{:S(2)}) copy-start(f32[1,320,2560]{2,1,0:T(8,128)} %param.15) | copy-start | bytes 9830404
  276.4 69.4 %collective-permute-start = (f32[320,2560]{1,0:T(8,128)}, f32[320,2560]{1,0:T(8,128)}, u32[]{:S(2)}, u32[]{:S(2)}) collective-permute-start(f32[320,2560]{1,0:T(8,128)} %param), channel_id=1, source_target_pairs={{0,16},{16,0},{32,48},{48,32},{64,80},{80,64},{96,112},{112,96},{1... | collective-permute-start | bytes 9830408 | tf_op jit(solution)/shard_map/cond/branch_0_fun/ppermute | solution.py:18
Sparse Core Ops, SparseCore 0:
  9.7 167.7 all-gather.2
where the time goes:
time: 362 us; the launch traced here: 361 us
  waiting for transfers between devices  207 us (57%)
  blocking collectives  55.2 us (15%)
  matrix products  43.6 us (12%)
  between operations  14.8 us (4%)
  local copies, waits for them, and re-layouts  14.7 us (4%)
  starting transfers between devices  14.1 us (4%)
  other arithmetic  11.6 us (3%)
    ppermute x1, waiting for transfers between devices, partner(): return lax.ppermute(value, axis, pairs)  67.5 us
    all_to_all x1, waiting for transfers between devices, per_device(): lax.all_to_all(cotangent[0], 'fsdp', split_axis=1, concat_axis=0, tiled=T...  55.3 us
    psum x1, blocking collectives, per_device(): lax.psum(jnp.sum(pre_norm * scaled, axis=1).astype(jnp.bfloat16), 'fsdp')  55.2 us
    all_to_all x1, waiting for transfers between devices, per_device(): lax.all_to_all(residual[0], 'fsdp', split_axis=1, concat_axis=0, tiled=True)  51.5 us
    all_gather x1, waiting for transfers between devices, per_device(): full_attn = lax.all_gather(local_attn, 'fsdp', axis=0, tiled=True)  32.3 us
    dot_general x1, matrix products, per_device(): lax.dot_general(full_attn, w_half, contract_feat, preferred_element_type=...  24.1 us
    dot_general x1, matrix products, per_device(): lax.dot_general(grad_pre, full_attn, contract_rows, preferred_element_typ...  19.5 us
    unnamed x6, local copies, waits for them, and re-layouts  8.77 us
  transfers between devices with their start and end apart: 4, of which 4 were waited for; matrix products, arithmetic and copies ran while one was open for 5% of the time, Pallas kernels for 0%

commit v1 on v0

--- a/solution.py
+++ b/solution.py
@@ -55,7 +55,8 @@
     w_half = params_local.astype(jnp.bfloat16)
     contract_feat = (((1,), (1,)), ((), ()))
     contract_rows = (((0,), (0,)), ((), ()))
-    full_attn = lax.all_gather(local_attn, "fsdp", axis=0, tiled=True)
+    r1 = jnp.stack(jax.lax.axis_size("fsdp") * [local_attn], axis=0)
+    full_attn = jnp.concatenate(jax.lax.all_to_all(r1, "fsdp", 0, 0), axis=0)
     pre_cols = lax.dot_general(full_attn, w_half, contract_feat, preferred_element_type=jnp.float32)
     resid_cols, cotan_cols = (
         lax.all_to_all(residual[0], "fsdp", split_axis=1, concat_axis=0, tiled=True),

time: 362 us -> 552 us (1.52)
  waiting for transfers between devices: 207 us -> 371 us
  blocking collectives: 55.2 us -> 90.4 us
  between operations: 14.8 us -> 1.47 us
  local copies, waits for them, and re-layouts: 14.7 us -> 20.6 us
    all_to_all x1, waiting for transfers between devices: 51.5 us -> 271 us  [per_device(): full_attn = jnp.concatenate(jax.lax.all_to_all(r1, 'fsdp', 0, 0), axis=0)]
    all_to_all x0 -> x1, blocking collectives: none -> 37.5 us  [per_device(): lax.all_to_all(residual[0], 'fsdp', split_axis=1, concat_axis=0, tiled=True)]
    all_gather x1 -> x0, waiting for transfers between devices: 32.3 us -> none  [per_device(): full_attn = lax.all_gather(local_attn, 'fsdp', axis=0, tiled=True)]
    all_to_all x1, waiting for transfers between devices: 55.3 us -> 32.3 us  [per_device(): lax.all_to_all(cotangent[0], 'fsdp', split_axis=1, concat_axis=0, tiled=T...]
    another operation x0 -> x1, local copies, waits for them, and re-layouts: none -> 7.36 us  [per_device(): r1 = jnp.stack(jax.lax.axis_size('fsdp') * [local_attn], axis=0)]
  transfers between devices with their start and end apart: 4 -> 3, of which waited for: 4 -> 3; matrix products, arithmetic and copies ran while one was open for 5% -> 2% of each run, Pallas kernels for 0% -> 0%
where the time goes in v1:
time: 552 us; the launch traced here: 551 us
  waiting for transfers between devices  371 us (67%)
  blocking collectives  90.4 us (16%)
  matrix products  43.7 us (8%)
  local copies, waits for them, and re-layouts  20.6 us (4%)
  starting transfers between devices  13 us (2%)
  other arithmetic  11.6 us (2%)
    all_to_all x1, waiting for transfers between devices, per_device(): full_attn = jnp.concatenate(jax.lax.all_to_all(r1, 'fsdp', 0, 0), axis=0)  271 us
    ppermute x1, waiting for transfers between devices, partner(): return lax.ppermute(value, axis, pairs)  67.5 us
    psum x1, blocking collectives, per_device(): lax.psum(jnp.sum(pre_norm * scaled, axis=1).astype(jnp.bfloat16), 'fsdp')  52.9 us
    all_to_all x1, blocking collectives, per_device(): lax.all_to_all(residual[0], 'fsdp', split_axis=1, concat_axis=0, tiled=True)  37.5 us
    all_to_all x1, waiting for transfers between devices, per_device(): lax.all_to_all(cotangent[0], 'fsdp', split_axis=1, concat_axis=0, tiled=T...  32.3 us
    dot_general x1, matrix products, per_device(): lax.dot_general(full_attn, w_half, contract_feat, preferred_element_type=...  24.2 us
    dot_general x1, matrix products, per_device(): lax.dot_general(grad_pre, full_attn, contract_rows, preferred_element_typ...  19.5 us
  transfers between devices with their start and end apart: 3, of which 3 were waited for; matrix products, arithmetic and copies ran while one was open for 2% of the time, Pallas kernels for 0%

profile of v1, /device:TPU:0, one launch (start us, length us, event | category | flops | bytes accessed | tf_op | source)
XLA Modules:
  0.0 551.4 jit_solution(15665954040739767595)
XLA Ops:
  0.6 4.4 copy.15
  5.0 5.6 %all-to-all-start.2 = ((bf16[256,16,320]{0,2,1:T(8,128)(2,1)}), bf16[256,16,320]{0,2,1:T(8,128)(2,1)}, u32[]{:S(2)}, u32[]{:S(2)}) async-start(bf16[256,16,320]{0,2,1:T(8,128)(2,1)} %bitcast.8), calls=%async_computation.2 | async-start | bytes 5242880 | tf_op jit(solution)/shard_map/all_to_all | solution.py:63
  10.6 3.0 copy.13
  13.6 32.3 %all-to-all-done.2 = bf16[256,16,320]{0,2,1:T(8,128)(2,1)} async-done(((bf16[256,16,320]{0,2,1:T(8,128)(2,1)}), bf16[256,16,320]{0,2,1:T(8,128)(2,1)}, u32[]{:S(2)}, u32[]{:S(2)}) %all-to-all-start.2) | async-done | bytes 2621472 | tf_op jit(solution)/shard_map/all_to_all | solution.py:63
  45.8 0.0 copy-start.2
  45.8 37.5 %all_to_all.31 = bf16[256,16,320]{0,2,1:T(8,128)(2,1)} all-to-all(bf16[256,16,320]{0,2,1:T(8,128)(2,1)S(1)} %bitcast.64), channel_id=1, replica_groups=mesh['rep'=8,'fsdp'=16] {'fsdp'}, dimensions={1} | all-to-all | bytes 5242880 | tf_op jit(solution)/shard_map/all_to_all | solution.py:62
  83.3 0.0 copy-done.2
  83.3 7.4 %stack.3 = bf16[16,256,2560]{2,1,0:T(8,128)(2,1)} broadcast(bf16[256,2560]{1,0:T(8,128)(2,1)S(1)} %bitcast.68), dimensions={1,2} | broadcast | bytes 22282240 | tf_op jit(solution)/shard_map/stack | solution.py:58
  90.7 0.0 copy-start.3
  90.7 5.5 all-to-all-start.1
  96.8 0.0 copy-done.3
  96.9 2.3 convert_bitcast_fusion
  99.2 0.0 copy-start
  99.3 3.0 copy.18
  102.2 0.0 copy-done
  102.2 0.6 convert_bitcast_fusion.1
  102.8 0.0 copy-start.1
  102.8 2.9 copy.17
  105.7 271.0 %all-to-all-done.1 = bf16[16,256,2560]{2,1,0:T(8,128)(2,1)} async-done(((bf16[16,256,2560]{2,1,0:T(8,128)(2,1)}), bf16[16,256,2560]{2,1,0:T(8,128)(2,1)}, u32[]{:S(2)}, u32[]{:S(2)}) %all-to-all-start.1) | async-done | bytes 20971552 | tf_op jit(solution)/shard_map/all_to_all | solution.py:59
  376.7 0.0 copy-done.1
  376.7 24.2 %multiply_reduce_fusion.1 = (bf16[4096]{0:T(1024)(128)(2,1)S(1)}, bf16[4096]{0:T(1024)(128)(2,1)S(1)}, f32[4096,320]{0,1:T(8,128)}) fusion(f32[4096,320]{0,1:T(8,128)} %bitcast.65, f32[320]{0:T(512)S(1)} %convert_element_type.53, f32[4096,320]{0,1:T(8,128)} %bitcast.67, bf16[4096,2560]{1,0:T(8,128)(2,1)} %bitcast.6, f32[1,320,2560]{2,1,0:T(8,128)S(1)} %copy-done.1), kind=kOutput, calls=%fused_computation.5 | convolution fusion | flops 6719561728 | bytes 39994624 | tf_op jit(solution)/shard_map/dot_general | solution.py:60
  400.8 52.9 %all-reduce = (bf16[4096]{0:T(1024)(128)(2,1)S(1)}, bf16[4096]{0:T(1024)(128)(2,1)S(1)}) all-reduce(bf16[4096]{0:T(1024)(128)(2,1)S(1)} %get-tuple-element.11, bf16[4096]{0:T(1024)(128)(2,1)S(1)} %get-tuple-element.10), channel_id=1, replica_groups=mesh['rep'=8,'fsdp'=16] {'fsdp'}, use_global_device_ids=true, to_apply=%region_3.0 | all-reduce | flops 8192 | bytes 32768 | tf_op jit(solution)/shard_map/psum | solution.py:71
  453.8 19.5 %bitcast_add_fusion.1 = (f32[320,2560]{1,0:T(8,128)}, f32[320,2560]{1,0:T(8,128)}) fusion(f32[1,320,2560]{2,1,0:T(8,128)S(1)} %copy-done.1, f32[]{:T(128)} %bitcast.12, f32[1,320,2560]{2,1,0:T(8,128)} %param.17, f32[]{:T(128)} %bitcast.10, f32[1,320,2560]{2,1,0:T(8,128)} %param.16, bf16[4096,2560]{1,0:T(8,128)(2,1)} %bitcast.6, ...), kind=kOutput, calls=%fused_computation.10 | convolution fusion | flops 6729728000 | bytes 47875336 | tf_op jit(solution)/shard_map/dot_general | solution.py:76
  473.3 69.4 %conditional.1 = (f32[320,2560]{1,0:T(8,128)}) conditional(s32[]{:T(128)} %clamp.3, f32[320,2560]{1,0:T(8,128)} %get-tuple-element.20, f32[320,2560]{1,0:T(8,128)} %get-tuple-element.20, f32[320,2560]{1,0:T(8,128)} %get-tuple-element.20), branch_computations={%region_4.5_spmd, %region_5.6_spmd, %region_6.7_spmd} | conditional | bytes 13107248 | solution.py:46
  473.3 1.9 collective-permute-start
  475.2 67.5 %collective-permute-done = f32[320,2560]{1,0:T(8,128)} collective-permute-done((f32[320,2560]{1,0:T(8,128)}, f32[320,2560]{1,0:T(8,128)}, u32[]{:S(2)}, u32[]{:S(2)}) %collective-permute-start) | collective-permute-done | bytes 3276832 | tf_op jit(solution)/shard_map/cond/branch_0_fun/ppermute | solution.py:18
  542.6 8.7 %fusion.12 = (f32[1,320,2560]{2,1,0:T(8,128)}, f32[1,320,2560]{2,1,0:T(8,128)}, f32[1,320,2560]{2,1,0:T(8,128)}) fusion(f32[320,2560]{1,0:T(8,128)} %get-tuple-element.21, f32[1,320,2560]{2,1,0:T(8,128)} %param.17, f32[]{:T(128)} %bitcast.12, f32[]{:T(128)} %bitcast.10, f32[1,320,2560]{2,1,0:T(8,128)} %param.16, f32[320,2560]{1,0:T(8,128)} %get-tuple-element.22, ...), kind=kLoop, calls=%fused_computation.23 | loop fusion | flops 13926400 | bytes 26214408 | tf_op jit(solution)/shard_map/broadcast_in_dim | solution.py:87
  (2 shorter events, 0.0 us)
Async XLA Ops:
  5.0 40.8 %all-to-all-start.2 = ((bf16[256,16,320]{0,2,1:T(8,128)(2,1)}), bf16[256,16,320]{0,2,1:T(8,128)(2,1)}, u32[]{:S(2)}, u32[]{:S(2)}) async-start(bf16[256,16,320]{0,2,1:T(8,128)(2,1)} %bitcast.8), calls=%async_computation.2 | async-start | bytes 5242880 | tf_op jit(solution)/shard_map/all_to_all | solution.py:63
  45.8 37.5 %copy-start.2 = (bf16[1,256,2560]{2,1,0:T(8,128)(2,1)S(1)}, bf16[1,256,2560]{2,1,0:T(8,128)(2,1)}, u32[]{:S(2)}) copy-start(bf16[1,256,2560]{2,1,0:T(8,128)(2,1)} %param.11) | copy-start | bytes 3932164
  90.7 6.1 %copy-start.3 = (bf16[320]{0:T(512)(128)(2,1)S(1)}, bf16[320]{0:T(512)(128)(2,1)}, u32[]{:S(2)}) copy-start(bf16[320]{0:T(512)(128)(2,1)} %param.14) | copy-start | bytes 1924
  90.7 286.0 %all-to-all-start.1 = ((bf16[16,256,2560]{2,1,0:T(8,128)(2,1)}), bf16[16,256,2560]{2,1,0:T(8,128)(2,1)}, u32[]{:S(2)}, u32[]{:S(2)}) async-start(bf16[16,256,2560]{2,1,0:T(8,128)(2,1)} %stack.3), calls=%async_computation.1 | async-start | bytes 41943040 | tf_op jit(solution)/shard_map/all_to_all | solution.py:59
  99.2 3.0 copy-start
  102.8 273.9 %copy-start.1 = (f32[1,320,2560]{2,1,0:T(8,128)S(1)}, f32[1,320,2560]{2,1,0:T(8,128)}, u32[]{:S(2)}) copy-start(f32[1,320,2560]{2,1,0:T(8,128)} %param.15) | copy-start | bytes 9830404
  473.3 69.4 %collective-permute-start = (f32[320,2560]{1,0:T(8,128)}, f32[320,2560]{1,0:T(8,128)}, u32[]{:S(2)}, u32[]{:S(2)}) collective-permute-start(f32[320,2560]{1,0:T(8,128)} %param), channel_id=1, source_target_pairs={{0,16},{16,0},{32,48},{48,32},{64,80},{80,64},{96,112},{112,96},{1... | collective-permute-start | bytes 9830408 | tf_op jit(solution)/shard_map/cond/branch_0_fun/ppermute | solution.py:18
